TPU v7x, 256 devices: a whole 4x4x8 slice. The times are simulated.
256 devices in a mesh: grp: 8 (over x_lo, y), slab: 32 (over x_hi, z, core).
Axes of the slice: x: 4 (x_hi: 2, x_lo: 2; x = x_hi * 2 + x_lo), y: 4, z: 8, core: 2. Of those that a mesh axis runs over, the one named last changes fastest.
Arguments:
- template: float32 [256, 64, 256], P('slab'), may hold values from -6 to 6
- images: bfloat16 [32, 256, 64, 256], P('grp', 'slab'), may hold values from -6 to 6
- velocity: float32 [32, 3, 256, 64, 256], P('grp', None, 'slab'), may hold values from -3 to 3
- labels: int32 [256, 64, 256], P('slab'), may hold values from 0 to 3
- stiffness: float32 [4], replicated, may hold values from 0.5 to 2
- cohort: int32 [32], P('grp'), may hold values from 0 to 7
- site_gain: float32 [8], replicated, may hold values from 0.5 to 2
Outputs:
- new_template: float32 [256, 64, 256], P('slab')
- new_velocity: float32 [32, 3, 256, 64, 256], P('grp', None, 'slab')
All inputs are finite; a program needn't handle non-finite values.
Results may differ from a plain program's by a relative error of at most 0.0003.
Values sent between devices are 32-bit elements; how exact they have to be, the bound alone decides.
No kernel may reach another device: no remote copies, remote signals or barrier semaphores. Data moves between devices by JAX's collectives and lax.ppermute only.
A program may use at most 64 MiB of HBM per device.

v0:
```python
import jax
import jax.numpy as jnp
from jax import lax
from jax.sharding import PartitionSpec as P

velocity_step = 0.05
template_step = 0.5


def extended(block, sides, width):
    for axis, dim in sides:
        count = lax.axis_size(axis)
        forward = [(i, i + 1) for i in range(count - 1)]
        backward = [(target, source) for source, target in forward]
        low = lax.ppermute(
            lax.slice_in_dim(block, block.shape[dim] - width, None, axis=dim), axis, forward
        )
        high = lax.ppermute(lax.slice_in_dim(block, 0, width, axis=dim), axis, backward)
        block = jnp.concatenate([low, block, high], axis=dim)
    return block


def slopes_of(padded):
    along_z = 0.5 * (padded[..., 2:, 1:-1, 1:-1] - padded[..., :-2, 1:-1, 1:-1])
    along_y = 0.5 * (padded[..., 1:-1, 2:, 1:-1] - padded[..., 1:-1, :-2, 1:-1])
    along_x = 0.5 * (padded[..., 1:-1, 1:-1, 2:] - padded[..., 1:-1, 1:-1, :-2])
    return jnp.stack([along_z, along_y, along_x], axis=-4)


def around_of(padded):
    beside_all = padded[..., 2:, 1:-1, 1:-1] + padded[..., :-2, 1:-1, 1:-1]
    beside_all = beside_all + padded[..., 1:-1, 2:, 1:-1] + padded[..., 1:-1, :-2, 1:-1]
    return beside_all + padded[..., 1:-1, 1:-1, 2:] + padded[..., 1:-1, 1:-1, :-2]


def pad_plane(field):
    return jnp.pad(field, [(0, 0)] * (field.ndim - 2) + [(1, 1), (1, 1)])


def local(template, images, velocity, labels, stiffness, cohort, site_gain):
    template_wide = extended(template, (("slab", 0),), 1)
    velocity_wide = extended(velocity, (("slab", 2),), 1)
    slopes = slopes_of(pad_plane(template_wide))
    levels = jnp.arange(stiffness.shape[0], dtype=jnp.int32)
    stiff_map = jnp.sum(
        jnp.where(labels[None] == levels[:, None, None, None], stiffness[:, None, None, None], 0.0),
        axis=0,
    )
    groups = jnp.arange(site_gain.shape[0], dtype=jnp.int32)
    subject_gain = jnp.sum(
        jnp.where(cohort[:, None] == groups[None, :], site_gain[None, :], 0.0), axis=1
    )
    warped = template[None] + jnp.sum(slopes[None] * velocity, axis=1)
    residual = warped - subject_gain[:, None, None, None] * images.astype(jnp.float32)
    elastic = stiff_map * (6.0 * velocity - around_of(pad_plane(velocity_wide)))
    new_velocity = velocity - velocity_step * (residual[:, None] * slopes[None] + elastic)
    group_partial = jnp.sum(residual, axis=0)
    subjects = images.shape[0] * lax.axis_size("grp")
    share = lax.psum_scatter(group_partial, "grp", scatter_dimension=1, tiled=True)
    share_rows = share.shape[1]
    own_rows = lax.dynamic_slice_in_dim(template, lax.axis_index("grp") * share_rows, share_rows, 1)
    new_template = lax.all_gather(
        own_rows - template_step * share / subjects, "grp", axis=1, tiled=True
    )
    return (new_template, new_velocity)


def solution(mesh):
    placed = (
        P("slab", None, None),
        P("grp", "slab", None, None),
        P("grp", None, "slab", None, None),
        P("slab", None, None),
        P(),
        P("grp"),
        P(),
    )
    return jax.shard_map(
        local,
        mesh=mesh,
        in_specs=placed,
        out_specs=(P("slab", None, None), P("grp", None, "slab", None, None)),
        check_vma=False,
    )
```

profile of v0, /device:TPU:4, one launch (start us, length us, event | category | flops | bytes accessed | tf_op | source)
XLA Modules:
  0.0 113.6 jit_solution(6247605921446230556)
XLA Ops:
  7.2 0.0 copy-start.2
  7.2 0.0 reduce-scatter.2.cloned.1.call-start
  7.2 0.9 fusion.21
  8.2 1.9 %collective-permute-start.1 = (f32[1,64,256]{2,1,0:T(8,128)S(1)}, f32[1,64,256]{2,1,0:T(8,128)S(1)}, u32[]{:S(2)}, u32[]{:S(2)}) collective-permute-start(f32[1,64,256]{2,1,0:T(8,128)S(1)} %get-tuple-element.8), channel_id=1, source_target_pairs={{0,1},{1,2},{2,3},{3,4},{4,5},{5,6},{6,7},{7,8},{8,9},{9,10},{10,1... | collective-permute-start | bytes 196616 | tf_op jit(solution)/shard_map/ppermute | solution.py:15
  10.1 7.3 %collective-permute-start = (f32[1,64,256]{2,1,0:T(8,128)S(1)}, f32[1,64,256]{2,1,0:T(8,128)S(1)}, u32[]{:S(2)}, u32[]{:S(2)}) collective-permute-start(f32[1,64,256]{2,1,0:T(8,128)S(1)} %get-tuple-element.9), channel_id=1, source_target_pairs={{1,0},{2,1},{3,2},{4,3},{5,4},{6,5},{7,6},{8,7},{9,8},{10,9},{11,1... | collective-permute-start | bytes 196616 | tf_op jit(solution)/shard_map/ppermute | solution.py:18
  17.3 2.7 %fusion.20 = (f32[4,3,1,64,256]{4,3,2,1,0:T(8,128)}, f32[4,3,1,64,256]{4,3,2,1,0:T(8,128)}) fusion(f32[4,3,8,64,256]{4,3,2,1,0:T(8,128)} %param.9), kind=kLoop, calls=%fused_computation.50 | loop fusion | bytes 3145728 | tf_op jit(solution)/shard_map/slice | solution.py:16
  20.0 1.9 %collective-permute-start.3 = (f32[4,3,1,64,256]{4,3,2,1,0:T(8,128)}, f32[4,3,1,64,256]{4,3,2,1,0:T(8,128)S(1)}, u32[]{:S(2)}, u32[]{:S(2)}) collective-permute-start(f32[4,3,1,64,256]{4,3,2,1,0:T(8,128)} %get-tuple-element.4), channel_id=1, source_target_pairs={{0,1},{1,2},{2,3},{3,4},{4,5},{5,6},{6,7},{7,8},{8,9},{9,10},{10,1... | collective-permute-start | bytes 2359304 | tf_op jit(solution)/shard_map/ppermute | solution.py:15
  22.0 7.3 %collective-permute-start.2 = (f32[4,3,1,64,256]{4,3,2,1,0:T(8,128)}, f32[4,3,1,64,256]{4,3,2,1,0:T(8,128)}, u32[]{:S(2)}, u32[]{:S(2)}) collective-permute-start(f32[4,3,1,64,256]{4,3,2,1,0:T(8,128)} %get-tuple-element.5), channel_id=1, source_target_pairs={{1,0},{2,1},{3,2},{4,3},{5,4},{6,5},{7,6},{8,7},{9,8},{10,9},{11,1... | collective-permute-start | bytes 2359304 | tf_op jit(solution)/shard_map/ppermute | solution.py:18
  29.2 0.0 copy-start
  29.2 1.5 %select_reduce_fusion = f32[8,64,256]{2,1,0:T(8,128)S(1)} fusion(f32[4]{0:T(128)} %param.11, s32[8,64,256]{2,1,0:T(8,128)} %param.10), kind=kLoop, calls=%fused_computation.22 | loop fusion | flops 1441792 | bytes 1048592 | tf_op jit(solution)/shard_map/reduce_sum | solution.py:45
  30.8 1.2 %select_reduce_fusion.1 = f32[4]{0:T(128)S(1)} fusion(f32[8]{0:T(128)} %param.13, s32[4]{0:T(128)} %param.12), kind=kLoop, calls=%fused_computation.47 | loop fusion | flops 92 | bytes 64 | tf_op jit(solution)/shard_map/reduce_sum | solution.py:50
  32.0 0.0 collective-permute-done.1
  32.0 0.0 collective-permute-done
  32.0 1.4 %select_maximum_fusion.2 = f32[10,66,258]{2,1,0:T(8,128)S(1)} fusion(f32[1,64,256]{2,1,0:T(8,128)S(1)} %collective-permute-done, f32[8,64,256]{2,1,0:T(8,128)} %param.7, f32[1,64,256]{2,1,0:T(8,128)S(1)} %collective-permute-done.1), kind=kLoop, calls=%fused_computation.30 | loop fusion | flops 2554200 | bytes 1336480 | tf_op jit(solution)/shard_map/concatenate | solution.py:19
  33.4 0.5 fusion.15
  33.9 0.0 copy-done.2
  34.0 0.0 copy-start.3
  34.0 0.1 pad_maximum_fusion.2
  34.1 0.0 copy-done
  34.1 1.1 multiply_reduce_fusion
  35.2 0.0 copy-done.3
  35.2 2.6 %fusion.19 = (f32[8,64,256]{2,1,0:T(8,128)}, f32[4,8,64,256]{3,2,1,0:T(8,128)}) fusion(bf16[4,8,64,256]{3,2,1,0:T(8,128)(2,1)S(1)} %copy-done.3, f32[4]{0:T(128)S(1)} %select_reduce_fusion.1, f32[4,8,64,256]{3,2,1,0:T(8,128)S(1)} %multiply_reduce_fusion, f32[8,64,256]{2,1,0:T(8,128)S(1)} %copy-done.2), kind=kLoop, calls=%fused_computation.49 | loop fusion | flops 2490368 | bytes 6291472 | tf_op jit(solution)/shard_map/reduce_sum | solution.py:57
  37.9 0.0 reduce-scatter.2.cloned.1.call-update
  37.9 0.0 copy-start.1
  37.9 0.0 collective-permute-done.3
  37.9 1.1 collective-permute-done.2
  39.0 7.6 %select_maximum_fusion = f32[4,3,10,66,258]{4,3,2,1,0:T(8,128)S(1)} fusion(f32[4,3,1,64,256]{4,3,2,1,0:T(8,128)} %collective-permute-done.2, f32[4,3,8,64,256]{4,3,2,1,0:T(8,128)} %param.9, f32[4,3,1,64,256]{4,3,2,1,0:T(8,128)S(1)} %collective-permute-done.3), kind=kLoop, calls=%fused_computation.4 | loop fusion | flops 30650400 | bytes 16037760 | tf_op jit(solution)/shard_map/concatenate | solution.py:19
  46.6 0.0 copy-done.1
  46.6 12.5 %fusion.7 = f32[4,3,8,64,256]{4,3,2,1,0:T(8,128)} fusion(f32[4,3,8,64,256]{4,3,2,1,0:T(8,128)} %param.9, f32[4,3,10,66,258]{4,3,2,1,0:T(8,128)S(1)} %select_maximum_fusion, f32[4,3,1,64,256]{4,3,2,1,0:T(8,128)S(1)} %collective-permute-done.3, f32[4,3,1,64,256]{4,3,2,1,0:T(8,128)} %collective-permute-done.2, f32[8,64,256]{2,1,0:T(8,128)S(1)} %select_reduce_fusion, ...), kind=kLoop, calls=%fused_computation.14 | loop fusion | flops 22020096 | bytes 43515904 | tf_op jit(solution)/shard_map/sub | solution.py:56
  59.1 17.0 %reduce-scatter.2.cloned.1.call-done = f32[8,8,256]{2,1,0:T(8,128)} async-done(((f32[8,64,256]{2,1,0:T(8,128)}), f32[8,8,256]{2,1,0:T(8,128)}) %reduce-scatter.2.cloned.1.call-update) | async-done | bytes 65552 | tf_op jit(solution)/shard_map/reduce_scatter | solution.py:59
  76.1 0.8 multiply_subtract_fusion.1
  77.0 29.0 %all_gather.3 = f32[8,64,256]{2,1,0:T(8,128)S(1)} all-gather(f32[8,8,256]{2,1,0:T(8,128)S(1)} %multiply_subtract_fusion.1), channel_id=1, replica_groups=mesh['grp'=8,'slab'=32] {'grp'}, dimensions={1}, use_global_device_ids=true | all-gather | bytes 589824 | tf_op jit(solution)/shard_map/all_gather | solution.py:62
  106.0 0.8 copy.10
  (1 shorter events, 0.0 us)
Async XLA Ops:
  7.2 26.8 %copy-start.2 = (f32[8,64,256]{2,1,0:T(8,128)S(1)}, f32[8,64,256]{2,1,0:T(8,128)}, u32[]{:S(2)}) copy-start(f32[8,64,256]{2,1,0:T(8,128)} %param.7) | copy-start | bytes 1572868
  7.2 68.9 %reduce-scatter.2.cloned.1.call-start = ((), (), s32[]{:S(2)}) async-start(), calls=%async_computation.1 | async-start | bytes 589824 | tf_op jit(solution)/shard_map/reduce_scatter | solution.py:59
  8.2 23.9 %collective-permute-start.1 = (f32[1,64,256]{2,1,0:T(8,128)S(1)}, f32[1,64,256]{2,1,0:T(8,128)S(1)}, u32[]{:S(2)}, u32[]{:S(2)}) collective-permute-start(f32[1,64,256]{2,1,0:T(8,128)S(1)} %get-tuple-element.8), channel_id=1, source_target_pairs={{0,1},{1,2},{2,3},{3,4},{4,5},{5,6},{6,7},{7,8},{8,9},{9,10},{10,1... | collective-permute-start | bytes 196616 | tf_op jit(solution)/shard_map/ppermute | solution.py:15
  10.1 21.9 %collective-permute-start = (f32[1,64,256]{2,1,0:T(8,128)S(1)}, f32[1,64,256]{2,1,0:T(8,128)S(1)}, u32[]{:S(2)}, u32[]{:S(2)}) collective-permute-start(f32[1,64,256]{2,1,0:T(8,128)S(1)} %get-tuple-element.9), channel_id=1, source_target_pairs={{1,0},{2,1},{3,2},{4,3},{5,4},{6,5},{7,6},{8,7},{9,8},{10,9},{11,1... | collective-permute-start | bytes 196616 | tf_op jit(solution)/shard_map/ppermute | solution.py:18
  20.0 17.9 %collective-permute-start.3 = (f32[4,3,1,64,256]{4,3,2,1,0:T(8,128)}, f32[4,3,1,64,256]{4,3,2,1,0:T(8,128)S(1)}, u32[]{:S(2)}, u32[]{:S(2)}) collective-permute-start(f32[4,3,1,64,256]{4,3,2,1,0:T(8,128)} %get-tuple-element.4), channel_id=1, source_target_pairs={{0,1},{1,2},{2,3},{3,4},{4,5},{5,6},{6,7},{7,8},{8,9},{9,10},{10,1... | collective-permute-start | bytes 2359304 | tf_op jit(solution)/shard_map/ppermute | solution.py:15
  22.0 17.1 %collective-permute-start.2 = (f32[4,3,1,64,256]{4,3,2,1,0:T(8,128)}, f32[4,3,1,64,256]{4,3,2,1,0:T(8,128)}, u32[]{:S(2)}, u32[]{:S(2)}) collective-permute-start(f32[4,3,1,64,256]{4,3,2,1,0:T(8,128)} %get-tuple-element.5), channel_id=1, source_target_pairs={{1,0},{2,1},{3,2},{4,3},{5,4},{6,5},{7,6},{8,7},{9,8},{10,9},{11,1... | collective-permute-start | bytes 2359304 | tf_op jit(solution)/shard_map/ppermute | solution.py:18
  29.2 4.9 %copy-start = (f32[4,3,8,64,256]{4,3,2,1,0:T(8,128)S(1)}, f32[4,3,8,64,256]{4,3,2,1,0:T(8,128)}, u32[]{:S(2)}) copy-start(f32[4,3,8,64,256]{4,3,2,1,0:T(8,128)} %param.9) | copy-start | bytes 18874372
  34.0 1.2 %copy-start.3 = (bf16[4,8,64,256]{3,2,1,0:T(8,128)(2,1)S(1)}, bf16[4,8,64,256]{3,2,1,0:T(8,128)(2,1)}, u32[]{:S(2)}) copy-start(bf16[4,8,64,256]{3,2,1,0:T(8,128)(2,1)} %param.8) | copy-start | bytes 3145732
  37.9 8.7 %copy-start.1 = (f32[4,8,64,256]{3,2,1,0:T(8,128)S(1)}, f32[4,8,64,256]{3,2,1,0:T(8,128)}, u32[]{:S(2)}) copy-start(f32[4,8,64,256]{3,2,1,0:T(8,128)} %get-tuple-element.3) | copy-start | bytes 6291460
Sparse Core Ops, SparseCore 0:
  38.0 38.0 reduce-scatter.1
where the time goes:
time: 114 us
  other arithmetic  29.5 us (26%)
  blocking collectives  29 us (25%)
  starting transfers between devices  18.4 us (16%)
  waiting for transfers between devices  18.1 us (16%)
  between operations  14.2 us (12%)
  local copies, waits for them, and re-layouts  4.45 us (4%)
    all_gather x1, blocking collectives, local(): lax.all_gather(own_rows - template_step * share / subjects, 'grp', axis=1...  29 us
    reduce_scatter x1, waiting for transfers between devices, local(): lax.psum_scatter(group_partial, 'grp', scatter_dimension=1, tiled=True)  17 us
    ppermute x2, starting transfers between devices, extended(): lax.ppermute(lax.slice_in_dim(block, 0, width, axis=dim), axis, backward)  14.5 us
    sub x1, other arithmetic, local(): velocity - velocity_step * (residual[:, None] * slopes[None] + elastic)  12.5 us
    concatenate x2, other arithmetic, extended(): block = jnp.concatenate([low, block, high], axis=dim)  8.97 us
    ppermute x2, starting transfers between devices, extended(): lax.ppermute(lax.slice_in_dim(block, block.shape[dim] - width, None, axis...  3.83 us
    slice x2, local copies, waits for them, and re-layouts, extended(): lax.slice_in_dim(block, block.shape[dim] - width, None, axis=dim)  3.62 us
    reduce_sum x1, other arithmetic, local(): group_partial = jnp.sum(residual, axis=0)  2.64 us
  transfers between devices with their start and end apart: 5, of which 2 were waited for; matrix products, arithmetic and copies ran while one was open for 28% of the time, Pallas kernels for 0%

commit v1 on v0

--- a/solution.py
+++ b/solution.py
@@ -5,6 +5,18 @@
 
 velocity_step = 0.05
 template_step = 0.5
+
+
+def _bind_sheets(array_in, dim_k):
+    return jnp.concatenate(
+        lax.all_to_all(
+            jnp.stack([array_in for _ in range(lax.axis_size("grp"))], axis=0),
+            axis_name="grp",
+            split_axis=0,
+            concat_axis=0,
+        ),
+        axis=dim_k,
+    )
 
 
 def extended(block, sides, width):
@@ -59,9 +71,7 @@
     share = lax.psum_scatter(group_partial, "grp", scatter_dimension=1, tiled=True)
     share_rows = share.shape[1]
     own_rows = lax.dynamic_slice_in_dim(template, lax.axis_index("grp") * share_rows, share_rows, 1)
-    new_template = lax.all_gather(
-        own_rows - template_step * share / subjects, "grp", axis=1, tiled=True
-    )
+    new_template = _bind_sheets(own_rows - template_step * share / subjects, 1)
     return (new_template, new_velocity)
 
 

time: 114 us -> 116 us (1.018)
  blocking collectives: 29 us -> 0 us
  other arithmetic: 29.5 us -> 45.8 us
  waiting for transfers between devices: 18.1 us -> 27.5 us
  starting transfers between devices: 18.4 us -> 21.9 us
    all_gather x1 -> x0, blocking collectives: 29 us -> none  [local(): lax.all_gather(own_rows - template_step * share / subjects, 'grp', axis=1...]
    sub x1, other arithmetic: 12.5 us -> 25.7 us  [local(): velocity - velocity_step * (residual[:, None] * slopes[None] + elastic)]
    reduce_scatter x1, waiting for transfers between devices: 17 us -> 26.3 us  [local(): lax.psum_scatter(group_partial, 'grp', scatter_dimension=1, tiled=True)]
    all_to_all x0 -> x1, starting transfers between devices: none -> 3.49 us  [_bind_sheets(): lax.all_to_all(jnp.stack([array_in for _ in range(lax.axis_size('grp'))],...]
    concatenate x2, other arithmetic: 8.97 us -> 12.2 us  [extended(): block = jnp.concatenate([low, block, high], axis=dim)]
  transfers between devices with their start and end apart: 5 -> 6, of which waited for: 2 -> 2; matrix products, arithmetic and copies ran while one was open for 28% -> 42% of each run, Pallas kernels for 0% -> 0%
where the time goes in v1:
time: 116 us; the launch traced here: 115 us
  other arithmetic  45.8 us (39%)
  waiting for transfers between devices  27.5 us (24%)
  starting transfers between devices  21.9 us (19%)
  between operations  14.2 us (12%)
  local copies, waits for them, and re-layouts  5.32 us (5%)
    reduce_scatter x1, waiting for transfers between devices, local(): lax.psum_scatter(group_partial, 'grp', scatter_dimension=1, tiled=True)  26.3 us
    sub x1, other arithmetic, local(): velocity - velocity_step * (residual[:, None] * slopes[None] + elastic)  25.7 us
    ppermute x2, starting transfers between devices, extended(): lax.ppermute(lax.slice_in_dim(block, 0, width, axis=dim), axis, backward)  14.5 us
    concatenate x2, other arithmetic, extended(): block = jnp.concatenate([low, block, high], axis=dim)  12.2 us
    ppermute x2, starting transfers between devices, extended(): lax.ppermute(lax.slice_in_dim(block, block.shape[dim] - width, None, axis...  3.83 us
    slice x2, local copies, waits for them, and re-layouts, extended(): lax.slice_in_dim(block, block.shape[dim] - width, None, axis=dim)  3.6 us
    all_to_all x1, starting transfers between devices, _bind_sheets(): lax.all_to_all(jnp.stack([array_in for _ in range(lax.axis_size('grp'))],...  3.49 us
    reduce_sum x1, other arithmetic, local(): group_partial = jnp.sum(residual, axis=0)  2.62 us
  transfers between devices with their start and end apart: 6, of which 2 were waited for; matrix products, arithmetic and copies ran while one was open for 42% of the time, Pallas kernels for 0%

profile of v1, /device:TPU:4, one launch (start us, length us, event | category | flops | bytes accessed | tf_op | source)
XLA Modules:
  0.0 114.7 jit_solution(17198903695313846229)
XLA Ops:
  7.2 0.0 copy-start.1
  7.2 0.0 reduce-scatter.2.cloned.1.call-start
  7.2 0.9 fusion.21
  8.2 1.9 %collective-permute-start.1 = (f32[1,64,256]{2,1,0:T(8,128)S(1)}, f32[1,64,256]{2,1,0:T(8,128)S(1)}, u32[]{:S(2)}, u32[]{:S(2)}) collective-permute-start(f32[1,64,256]{2,1,0:T(8,128)S(1)} %get-tuple-element.8), channel_id=1, source_target_pairs={{0,1},{1,2},{2,3},{3,4},{4,5},{5,6},{6,7},{7,8},{8,9},{9,10},{10,1... | collective-permute-start | bytes 196616 | tf_op jit(solution)/shard_map/ppermute | solution.py:27
  10.1 7.3 %collective-permute-start = (f32[1,64,256]{2,1,0:T(8,128)S(1)}, f32[1,64,256]{2,1,0:T(8,128)S(1)}, u32[]{:S(2)}, u32[]{:S(2)}) collective-permute-start(f32[1,64,256]{2,1,0:T(8,128)S(1)} %get-tuple-element.9), channel_id=1, source_target_pairs={{1,0},{2,1},{3,2},{4,3},{5,4},{6,5},{7,6},{8,7},{9,8},{10,9},{11,1... | collective-permute-start | bytes 196616 | tf_op jit(solution)/shard_map/ppermute | solution.py:30
  17.3 2.7 %fusion.20 = (f32[4,3,1,64,256]{4,3,2,1,0:T(8,128)}, f32[4,3,1,64,256]{4,3,2,1,0:T(8,128)}) fusion(f32[4,3,8,64,256]{4,3,2,1,0:T(8,128)} %param.9), kind=kLoop, calls=%fused_computation.51 | loop fusion | bytes 3145728 | tf_op jit(solution)/shard_map/slice | solution.py:28
  20.0 1.9 %collective-permute-start.3 = (f32[4,3,1,64,256]{4,3,2,1,0:T(8,128)}, f32[4,3,1,64,256]{4,3,2,1,0:T(8,128)S(1)}, u32[]{:S(2)}, u32[]{:S(2)}) collective-permute-start(f32[4,3,1,64,256]{4,3,2,1,0:T(8,128)} %get-tuple-element.4), channel_id=1, source_target_pairs={{0,1},{1,2},{2,3},{3,4},{4,5},{5,6},{6,7},{7,8},{8,9},{9,10},{10,1... | collective-permute-start | bytes 2359304 | tf_op jit(solution)/shard_map/ppermute | solution.py:27
  21.9 7.3 %collective-permute-start.2 = (f32[4,3,1,64,256]{4,3,2,1,0:T(8,128)}, f32[4,3,1,64,256]{4,3,2,1,0:T(8,128)}, u32[]{:S(2)}, u32[]{:S(2)}) collective-permute-start(f32[4,3,1,64,256]{4,3,2,1,0:T(8,128)} %get-tuple-element.5), channel_id=1, source_target_pairs={{1,0},{2,1},{3,2},{4,3},{5,4},{6,5},{7,6},{8,7},{9,8},{10,9},{11,1... | collective-permute-start | bytes 2359304 | tf_op jit(solution)/shard_map/ppermute | solution.py:30
  29.2 0.0 copy-start
  29.2 1.5 %select_reduce_fusion = f32[8,64,256]{2,1,0:T(8,128)S(1)} fusion(f32[4]{0:T(128)} %param.11, s32[8,64,256]{2,1,0:T(8,128)} %param.10), kind=kLoop, calls=%fused_computation.22 | loop fusion | flops 1441792 | bytes 1048592 | tf_op jit(solution)/shard_map/reduce_sum | solution.py:57
  30.8 1.2 %select_reduce_fusion.1 = f32[4]{0:T(128)S(1)} fusion(f32[8]{0:T(128)} %param.13, s32[4]{0:T(128)} %param.12), kind=kLoop, calls=%fused_computation.48 | loop fusion | flops 92 | bytes 64 | tf_op jit(solution)/shard_map/reduce_sum | solution.py:62
  32.0 0.0 collective-permute-done.1
  32.0 0.0 collective-permute-done
  32.0 1.4 %select_maximum_fusion.2 = f32[10,66,258]{2,1,0:T(8,128)S(1)} fusion(f32[1,64,256]{2,1,0:T(8,128)S(1)} %collective-permute-done, f32[8,64,256]{2,1,0:T(8,128)} %param.7, f32[1,64,256]{2,1,0:T(8,128)S(1)} %collective-permute-done.1), kind=kLoop, calls=%fused_computation.30 | loop fusion | flops 2554200 | bytes 1336480 | tf_op jit(solution)/shard_map/concatenate | solution.py:31
  33.4 0.5 fusion.15
  33.9 0.0 copy-done.1
  34.0 0.0 copy-start.2
  34.0 0.1 pad_maximum_fusion.2
  34.1 0.0 copy-done
  34.1 1.1 multiply_reduce_fusion
  35.2 0.0 copy-done.2
  35.2 2.6 %fusion.19 = (f32[8,64,256]{2,1,0:T(8,128)}, f32[4,8,64,256]{3,2,1,0:T(8,128)}) fusion(bf16[4,8,64,256]{3,2,1,0:T(8,128)(2,1)S(1)} %copy-done.2, f32[4]{0:T(128)S(1)} %select_reduce_fusion.1, f32[4,8,64,256]{3,2,1,0:T(8,128)S(1)} %multiply_reduce_fusion, f32[8,64,256]{2,1,0:T(8,128)S(1)} %copy-done.1), kind=kLoop, calls=%fused_computation.50 | loop fusion | flops 2490368 | bytes 6291472 | tf_op jit(solution)/shard_map/reduce_sum | solution.py:69
  37.8 0.0 reduce-scatter.2.cloned.1.call-update
  37.8 0.0 collective-permute-done.3
  37.9 1.1 collective-permute-done.2
  39.0 10.8 %select_maximum_fusion = f32[4,3,10,66,258]{4,3,2,1,0:T(8,128)} fusion(f32[4,3,1,64,256]{4,3,2,1,0:T(8,128)} %collective-permute-done.2, f32[4,3,8,64,256]{4,3,2,1,0:T(8,128)} %param.9, f32[4,3,1,64,256]{4,3,2,1,0:T(8,128)S(1)} %collective-permute-done.3), kind=kLoop, calls=%fused_computation.4 | loop fusion | flops 30650400 | bytes 16037760 | tf_op jit(solution)/shard_map/concatenate | solution.py:31
  49.8 26.3 %reduce-scatter.2.cloned.1.call-done = f32[8,8,256]{2,1,0:T(8,128)} async-done(((f32[8,64,256]{2,1,0:T(8,128)}), f32[8,8,256]{2,1,0:T(8,128)}) %reduce-scatter.2.cloned.1.call-update) | async-done | bytes 65552 | tf_op jit(solution)/shard_map/reduce_scatter | solution.py:71
  76.1 0.8 multiply_subtract_fusion.1
  76.9 0.8 stack.27
  77.8 3.5 %all-to-all-start = ((f32[8,8,8,256]{3,2,1,0:T(8,128)}), f32[8,8,8,256]{3,2,1,0:T(8,128)S(1)}, u32[]{:S(2)}, u32[]{:S(2)}) async-start(f32[8,8,8,256]{3,2,1,0:T(8,128)} %stack.27), calls=%async_computation.1 | async-start | bytes 1048576 | tf_op jit(solution)/shard_map/all_to_all | solution.py:12
  81.3 25.7 %fusion.7 = f32[4,3,8,64,256]{4,3,2,1,0:T(8,128)} fusion(f32[4,3,8,64,256]{4,3,2,1,0:T(8,128)} %param.9, f32[4,3,10,66,258]{4,3,2,1,0:T(8,128)} %select_maximum_fusion, f32[4,3,1,64,256]{4,3,2,1,0:T(8,128)S(1)} %collective-permute-done.3, f32[4,3,1,64,256]{4,3,2,1,0:T(8,128)} %collective-permute-done.2, f32[8,64,256]{2,1,0:T(8,128)S(1)} %select_reduce_fusion, ...), kind=kLoop, calls=%fused_computation.14 | loop fusion | flops 22020096 | bytes 43515904 | tf_op jit(solution)/shard_map/sub | solution.py:68
  107.0 0.0 all-to-all-done
  107.0 0.8 copy.12
  (1 shorter events, 0.0 us)
Async XLA Ops:
  7.2 26.7 %copy-start.1 = (f32[8,64,256]{2,1,0:T(8,128)S(1)}, f32[8,64,256]{2,1,0:T(8,128)}, u32[]{:S(2)}) copy-start(f32[8,64,256]{2,1,0:T(8,128)} %param.7) | copy-start | bytes 1572868
  7.2 68.9 %reduce-scatter.2.cloned.1.call-start = ((), (), s32[]{:S(2)}) async-start(), calls=%async_computation.2 | async-start | bytes 589824 | tf_op jit(solution)/shard_map/reduce_scatter | solution.py:71
  8.2 23.8 %collective-permute-start.1 = (f32[1,64,256]{2,1,0:T(8,128)S(1)}, f32[1,64,256]{2,1,0:T(8,128)S(1)}, u32[]{:S(2)}, u32[]{:S(2)}) collective-permute-start(f32[1,64,256]{2,1,0:T(8,128)S(1)} %get-tuple-element.8), channel_id=1, source_target_pairs={{0,1},{1,2},{2,3},{3,4},{4,5},{5,6},{6,7},{7,8},{8,9},{9,10},{10,1... | collective-permute-start | bytes 196616 | tf_op jit(solution)/shard_map/ppermute | solution.py:27
  10.1 21.9 %collective-permute-start = (f32[1,64,256]{2,1,0:T(8,128)S(1)}, f32[1,64,256]{2,1,0:T(8,128)S(1)}, u32[]{:S(2)}, u32[]{:S(2)}) collective-permute-start(f32[1,64,256]{2,1,0:T(8,128)S(1)} %get-tuple-element.9), channel_id=1, source_target_pairs={{1,0},{2,1},{3,2},{4,3},{5,4},{6,5},{7,6},{8,7},{9,8},{10,9},{11,1... | collective-permute-start | bytes 196616 | tf_op jit(solution)/shard_map/ppermute | solution.py:30
  20.0 17.8 %collective-permute-start.3 = (f32[4,3,1,64,256]{4,3,2,1,0:T(8,128)}, f32[4,3,1,64,256]{4,3,2,1,0:T(8,128)S(1)}, u32[]{:S(2)}, u32[]{:S(2)}) collective-permute-start(f32[4,3,1,64,256]{4,3,2,1,0:T(8,128)} %get-tuple-element.4), channel_id=1, source_target_pairs={{0,1},{1,2},{2,3},{3,4},{4,5},{5,6},{6,7},{7,8},{8,9},{9,10},{10,1... | collective-permute-start | bytes 2359304 | tf_op jit(solution)/shard_map/ppermute | solution.py:27
  21.9 17.1 %collective-permute-start.2 = (f32[4,3,1,64,256]{4,3,2,1,0:T(8,128)}, f32[4,3,1,64,256]{4,3,2,1,0:T(8,128)}, u32[]{:S(2)}, u32[]{:S(2)}) collective-permute-start(f32[4,3,1,64,256]{4,3,2,1,0:T(8,128)} %get-tuple-element.5), channel_id=1, source_target_pairs={{1,0},{2,1},{3,2},{4,3},{5,4},{6,5},{7,6},{8,7},{9,8},{10,9},{11,1... | collective-permute-start | bytes 2359304 | tf_op jit(solution)/shard_map/ppermute | solution.py:30
  29.2 4.9 %copy-start = (f32[4,3,8,64,256]{4,3,2,1,0:T(8,128)S(1)}, f32[4,3,8,64,256]{4,3,2,1,0:T(8,128)}, u32[]{:S(2)}) copy-start(f32[4,3,8,64,256]{4,3,2,1,0:T(8,128)} %param.9) | copy-start | bytes 18874372
  34.0 1.2 %copy-start.2 = (bf16[4,8,64,256]{3,2,1,0:T(8,128)(2,1)S(1)}, bf16[4,8,64,256]{3,2,1,0:T(8,128)(2,1)}, u32[]{:S(2)}) copy-start(bf16[4,8,64,256]{3,2,1,0:T(8,128)(2,1)} %param.8) | copy-start | bytes 3145732
  77.8 29.2 %all-to-all-start = ((f32[8,8,8,256]{3,2,1,0:T(8,128)}), f32[8,8,8,256]{3,2,1,0:T(8,128)S(1)}, u32[]{:S(2)}, u32[]{:S(2)}) async-start(f32[8,8,8,256]{3,2,1,0:T(8,128)} %stack.27), calls=%async_computation.1 | async-start | bytes 1048576 | tf_op jit(solution)/shard_map/all_to_all | solution.py:12
Sparse Core Ops, SparseCore 0:
  38.0 38.0 reduce-scatter.1
